TPU v7x, 128 devices: a whole 4x4x4 slice. The times are simulated.
128 devices in a mesh: row: 8 (over x, core), col: 16 (over z, y).
Axes of the slice: x: 4, y: 4, z: 4, core: 2. Of those that a mesh axis runs over, the one named last changes fastest.
Arguments:
- tokens: bfloat16 [7168, 4096], P('col', 'row'), may hold values from -50 to 50
- ln_gain: float32 [4096], P('row'), may hold values from 0.1 to 1.9
- ln_shift: float32 [4096], P('row'), may hold values from -4 to 4
- w_qkv: bfloat16 [4096, 12288], P('row', 'col'), may hold values from -2 to 2
- w_out: bfloat16 [4096, 4096], P('col', 'row'), may hold values from -0.09375 to 0.09375
- layer_scale: float32 [4096], P('row'), may hold values from 0.5 to 2
- segments: int32 [7168], replicated, may hold values from 0 to 16, as said below
- present: int32 [7168], replicated, may hold values from 0 to 1, as said below
- coords: int32 [2, 7168], replicated, may hold values from 0 to 22, as said below
- owner_slot: int32 [7168], replicated, may hold values from 0 to 7167, as said below
Outputs:
- layer_out: bfloat16 [7168, 4096], P('col', 'row')
Inputs may be any that keep to these rules, and one draw needn't show every extreme that they name: `segments`: the picture of each token, pictures numbered in stream order; each picture's tokens form one run, pictures follow each other from position 0, and the padding tokens after them carry 16. `present`: 1 exactly where segments is below 16. A picture has h rows of w patches, 8 <= h <= 18 and 12 <= w <= 22, and some picture has 18 rows of 22; its first 5 tokens (class and registers) have 0 in both rows of coords, then its patches follow in row-major order with patch row and column counted from 1; padding tokens have 0 in both. `owner_slot`: A permutation of the 7168 tokens onto slots. Each block of 896 slots (slot // 896) holds 2 whole pictures, each on consecutive slots in stream order, followed by padding tokens.
All inputs are finite; a program needn't handle non-finite values.
Results may differ from a plain program's by a relative error of at most 0.017.
Values may be sent and summed in bfloat16 or wider, within the bound.
A program may use at most 64 MiB of HBM per device.

v0:
```python
import jax
import jax.numpy as jnp
from jax import lax
from jax.sharding import PartitionSpec as P

D = 4096
HD = 128


def rotate(values, row_pos, col_pos):
    quarter = values.shape[-1] // 4
    frequency = 100.0 ** (-jnp.arange(quarter, dtype=jnp.float32) / quarter)
    angles = jnp.concatenate(
        [row_pos[:, None] * frequency[None, :], col_pos[:, None] * frequency[None, :]], axis=1
    )
    cosine = jnp.cos(angles)[:, None, :]
    sine_wave = jnp.sin(angles)[:, None, :]
    former = jnp.concatenate(
        [values[..., :quarter], values[..., 2 * quarter : 3 * quarter]], axis=-1
    )
    latter = jnp.concatenate(
        [values[..., quarter : 2 * quarter], values[..., 3 * quarter :]], axis=-1
    )
    new_former = former * cosine - latter * sine_wave
    new_latter = latter * cosine + former * sine_wave
    return jnp.concatenate(
        [
            new_former[..., :quarter],
            new_latter[..., :quarter],
            new_former[..., quarter:],
            new_latter[..., quarter:],
        ],
        axis=-1,
    )


def normalize(values, totals, squares, ln_gain, ln_shift):
    average = totals / D
    spread = squares / D - average * average
    scale_inv = lax.rsqrt(spread + 1e-06)
    return ((values - average[:, None]) * scale_inv[:, None] * ln_gain + ln_shift).astype(
        jnp.bfloat16
    )


def local(
    tokens, ln_gain, ln_shift, w_qkv, w_out, layer_scale, segments, present, coords, owner_slot
):
    own_rows = tokens.astype(jnp.float32)
    totals, squares = lax.psum(
        (jnp.sum(own_rows, axis=1), jnp.sum(own_rows * own_rows, axis=1)), "row"
    )
    normed = normalize(own_rows, totals, squares, ln_gain, ln_shift)
    gathered = lax.all_gather(normed, "col", axis=0, tiled=True)
    slot_count = owner_slot.shape[0]
    at_slot = (
        jnp.zeros((slot_count,), jnp.int32)
        .at[owner_slot]
        .set(jnp.arange(slot_count, dtype=jnp.int32))
    )
    placed = gathered[at_slot]
    group_rows = slot_count // lax.axis_size("row")
    mixed = lax.psum_scatter(
        jnp.dot(placed, w_qkv, preferred_element_type=jnp.float32).astype(jnp.bfloat16),
        "row",
        scatter_dimension=0,
        tiled=True,
    ).astype(jnp.float32)
    heads_here = w_qkv.shape[1] // (3 * HD)
    mixed = mixed.reshape(group_rows, heads_here, 3, HD)
    my_slots = lax.dynamic_slice_in_dim(at_slot, lax.axis_index("row") * group_rows, group_rows, 0)
    row_pos = coords[0][my_slots].astype(jnp.float32)
    col_pos = coords[1][my_slots].astype(jnp.float32)
    seg_rows = segments[my_slots]
    live_rows = present[my_slots]
    query_rows = rotate(mixed[:, :, 0], row_pos, col_pos).astype(jnp.bfloat16)
    key_rows = rotate(mixed[:, :, 1], row_pos, col_pos).astype(jnp.bfloat16)
    values = mixed[:, :, 2].astype(jnp.bfloat16)
    scores = jnp.einsum(
        "qhe,khe->hqk", query_rows, key_rows, preferred_element_type=jnp.float32
    ) * HD ** (-0.5)
    allowed = (seg_rows[:, None] == seg_rows[None, :]) & (live_rows[None, :] == 1)
    scores = jnp.where(allowed[None], scores, -1e30)
    highest = jnp.max(scores, axis=-1, keepdims=True)
    weights = jnp.exp(scores - highest)
    probability = (weights / jnp.sum(weights, axis=-1, keepdims=True)).astype(jnp.bfloat16)
    result = jnp.einsum("hqk,khe->qhe", probability, values, preferred_element_type=jnp.float32)
    attended = (result * live_rows[:, None, None].astype(jnp.float32)).astype(jnp.bfloat16)
    attended = attended.reshape(group_rows, heads_here * HD)
    all_slots = lax.all_gather(attended, "row", axis=0, tiled=True)
    projected = lax.psum_scatter(
        jnp.dot(all_slots[owner_slot], w_out, preferred_element_type=jnp.float32).astype(
            jnp.bfloat16
        ),
        "col",
        scatter_dimension=0,
        tiled=True,
    ).astype(jnp.float32)
    return (own_rows + layer_scale * projected).astype(jnp.bfloat16)


def solution(mesh):
    in_specs = (
        P("col", "row"),
        P("row"),
        P("row"),
        P("row", "col"),
        P("col", "row"),
        P("row"),
        P(),
        P(),
        P(),
        P(),
    )
    out_specs = P("col", "row")
    return jax.shard_map(local, mesh=mesh, in_specs=in_specs, out_specs=out_specs, check_vma=False)
```

profile of v0, /device:TPU:1, one launch (start us, length us, event | category | flops | bytes accessed | tf_op | source)
XLA Modules:
  0.0 381.5 jit_solution(2450484847062370602)
XLA Ops:
  6.5 0.0 copy-start
  6.5 0.0 all-gather.3.cloned.1.call-start
  6.5 1.3 convert_reduce_fusion
  7.9 13.2 %all-reduce = (f32[448]{0:T(512)S(1)}, f32[448]{0:T(512)S(1)}) all-reduce(f32[448]{0:T(512)S(1)} %get-tuple-element.6, f32[448]{0:T(512)S(1)} %get-tuple-element.5), channel_id=1, replica_groups=mesh['row'=8,'col'=16] {'row'}, use_global_device_ids=true, to_apply=%region_3.0 | all-reduce | flops 896 | bytes 7168 | tf_op jit(solution)/shard_map/psum | solution.py:50
  21.1 2.0 fusion.11
  23.1 0.0 all-gather.3.cloned.1.call-update
  23.1 0.0 reduce-scatter.3.cloned.1.call-start
  23.2 1.4 broadcast_clamp_fusion
  24.6 26.8 %scatter_custom_fusion = s32[7168]{0:T(1024)S(1)} fusion(s32[7168]{0:T(1024)S(1)} %get-tuple-element.38, s32[7168]{0:T(1024)S(1)} %iota.11, s32[]{:T(128)} %constant.17.clone.1), kind=kCustom, calls=%fused_computation.54 | custom fusion | bytes 28676 | tf_op jit(solution)/shard_map/scatter | solution.py:59
  51.3 40.2 %all-gather.3.cloned.1.call-done = bf16[7168,512]{1,0:T(8,128)(2,1)} async-done(((bf16[448,512]{1,0:T(8,128)(2,1)}), bf16[7168,512]{1,0:T(8,128)(2,1)}) %all-gather.3.cloned.1.call-update) | async-done | bytes 7340048 | tf_op jit(solution)/shard_map/all_gather | solution.py:54
  91.5 33.8 %gather_fusion = bf16[7168,512]{1,0:T(8,128)(2,1)} fusion(bf16[7168,512]{1,0:T(8,128)(2,1)} %all-gather.3.cloned.1.call-done, s32[7168]{0:T(1024)S(1)} %fusion.18), kind=kCustom, calls=%fused_computation | custom fusion | bytes 14708736 | tf_op jit(solution)/shard_map/gather | solution.py:61
  125.3 0.0 copy-done
  125.3 11.4 %convolution_convert_fusion = bf16[7168,768]{1,0:T(8,128)(2,1)} fusion(bf16[7168,512]{1,0:T(8,128)(2,1)} %gather_fusion, bf16[512,768]{1,0:T(8,128)(2,1)S(1)} %copy-done), kind=kOutput, calls=%fused_computation.8 | convolution fusion | flops 5642649600 | bytes 19136512 | tf_op jit(solution)/shard_map/dot_general | solution.py:64
  136.7 0.0 copy-start.10
  136.7 0.0 reduce-scatter.3.cloned.1.call-update
  136.7 0.0 copy-start.2
  136.7 0.0 copy-start.3
  136.7 0.2 all-gather.5.cloned.1.call-start
  137.0 0.1 compare_select_fusion.2
  137.1 0.4 copy-done.10
  137.6 5.2 %gather_fusion.3 = s32[896]{0:T(1024)S(1)} fusion(s32[7168]{0:T(1024)S(1)} %bitcast.20, s32[1024]{0:T(1024)S(1)} %pad_clamp_fusion), kind=kCustom, calls=%fused_computation.3 | custom fusion | bytes 10752 | tf_op jit(solution)/shard_map/gather | solution.py:72
  142.7 5.2 %gather_fusion.4 = s32[896]{0:T(1024)S(1)} fusion(s32[7168]{0:T(1024)S(1)} %bitcast.19, s32[1024]{0:T(1024)S(1)} %pad_clamp_fusion), kind=kCustom, calls=%fused_computation.4 | custom fusion | bytes 10752 | tf_op jit(solution)/shard_map/gather | solution.py:73
  147.9 0.0 copy-done.2
  147.9 5.2 %gather_fusion.2 = s32[896]{0:T(1024)S(1)} fusion(s32[7168]{0:T(1024)S(1)} %copy-done.2, s32[1024]{0:T(1024)S(1)} %pad_clamp_fusion), kind=kCustom, calls=%fused_computation.2 | custom fusion | bytes 10752 | tf_op jit(solution)/shard_map/gather | solution.py:75
  153.1 0.0 copy-done.3
  153.1 5.2 %gather_fusion.1 = s32[896]{0:T(1024)S(1)} fusion(s32[7168]{0:T(1024)S(1)} %copy-done.3, s32[1024]{0:T(1024)S(1)} %pad_clamp_fusion), kind=kCustom, calls=%fused_computation.1 | custom fusion | bytes 10752 | tf_op jit(solution)/shard_map/gather | solution.py:74
  158.3 0.3 broadcast_multiply_fusion.1
  158.6 2.6 fusion.17
  161.2 1.6 compare_and_fusion
  162.8 38.2 %reduce-scatter.3.cloned.1.call-done = bf16[896,768]{1,0:T(8,128)(2,1)} async-done(((bf16[7168,768]{1,0:T(8,128)(2,1)}), bf16[896,768]{1,0:T(8,128)(2,1)}) %reduce-scatter.3.cloned.1.call-update) | async-done | bytes 1376272 | tf_op jit(solution)/shard_map/reduce_scatter | solution.py:63
  201.0 1.8 copy.15
  202.8 0.8 copy.17
  203.6 0.2 reshape.134
  203.8 0.1 slice_bitcast_fusion
  203.9 0.0 copy-start.5
  204.0 0.0 copy-start.6
  204.0 1.5 fusion.23
  205.5 0.0 copy-done.5
  205.5 0.0 copy-done.6
  205.5 0.0 copy-start.7
  205.5 1.0 subtract_convert_fusion
  206.6 1.0 fusion.25
  207.5 1.1 fusion.26
  208.6 1.2 fusion.27
  209.8 1.1 fusion.28
  210.9 0.0 copy-done.7
  210.9 7.9 %fusion.30 = (f32[2,896]{1,0:T(2,128)S(1)}, f32[2,896,896]{1,2,0:T(8,128)}) fusion(pred[896,896]{0,1:T(8,128)(4,1)S(1)} %copy-done.7, bf16[896,2,32]{2,0,1:T(8,128)(2,1)} %get-tuple-element.30, bf16[896,2,32]{2,0,1:T(8,128)(2,1)} %get-tuple-element.28, bf16[896,2,32]{2,0,1:T(8,128)(2,1)} %get-tuple-element.29, ...), kind=kOutput, calls=%fused_computation.71 | convolution fusion | flops 421135232 | bytes 8150016 | tf_op jit(solution)/shard_map/sub | solution.py:85
  218.8 0.0 copy-start.9
  218.8 3.6 fusion.7
  222.3 1.0 copy.19
  223.3 0.0 all-gather.5.cloned.1.call-update
  223.3 0.3 reduce-scatter.5.cloned.1.call-start
  223.6 30.3 %all-gather.5.cloned.1.call-done = bf16[7168,256]{1,0:T(8,128)(2,1)} async-done(((bf16[896,256]{1,0:T(8,128)(2,1)}), bf16[7168,256]{1,0:T(8,128)(2,1)}) %all-gather.5.cloned.1.call-update) | async-done | bytes 3670032 | tf_op jit(solution)/shard_map/all_gather | solution.py:90
  253.9 0.0 copy-done.9
  253.9 0.0 copy-start.8
  253.9 29.8 %gather_fusion.5 = bf16[7168,256]{1,0:T(8,128)(2,1)} fusion(bf16[7168,256]{1,0:T(8,128)(2,1)} %all-gather.5.cloned.1.call-done, s32[7168]{0:T(1024)S(1)} %copy-done.9), kind=kCustom, calls=%fused_computation.5 | custom fusion | bytes 7368704 | tf_op jit(solution)/shard_map/gather | solution.py:92
  283.7 0.0 copy-done.8
  283.7 7.1 %convolution_convert_fusion.1 = bf16[7168,512]{1,0:T(8,128)(2,1)} fusion(bf16[7168,256]{1,0:T(8,128)(2,1)} %gather_fusion.5, bf16[256,512]{1,0:T(8,128)(2,1)S(1)} %copy-done.8), kind=kOutput, calls=%fused_computation.9 | convolution fusion | flops 1882718208 | bytes 11272192 | tf_op jit(solution)/shard_map/dot_general | solution.py:92
  290.8 0.0 reduce-scatter.5.cloned.1.call-update
  290.8 82.2 %reduce-scatter.5.cloned.1.call-done = bf16[448,512]{1,0:T(8,128)(2,1)} async-done(((bf16[7168,512]{1,0:T(8,128)(2,1)}), bf16[448,512]{1,0:T(8,128)(2,1)}) %reduce-scatter.5.cloned.1.call-update) | async-done | bytes 458768 | tf_op jit(solution)/shard_map/reduce_scatter | solution.py:91
  373.0 0.0 copy-done.4
  373.0 0.0 copy-done.11
  373.0 1.9 fusion.13
  374.9 0.0 copy-done.1
  (13 shorter events, 0.1 us)
Async XLA Ops:
  6.5 118.8 %copy-start = (bf16[512,768]{1,0:T(8,128)(2,1)S(1)}, bf16[512,768]{1,0:T(8,128)(2,1)}, u32[]{:S(2)}) copy-start(bf16[512,768]{1,0:T(8,128)(2,1)} %param.13) | copy-start | bytes 2359300
  6.5 85.0 %all-gather.3.cloned.1.call-start = ((), (), s32[]{:S(2)}) async-start(), calls=%async_computation.2 | async-start | bytes 7798784 | tf_op jit(solution)/shard_map/all_gather | solution.py:54
  23.1 177.8 %reduce-scatter.3.cloned.1.call-start = ((), (), s32[]{:S(2)}) async-start(), calls=%async_computation.3 | async-start | bytes 12386304 | tf_op jit(solution)/shard_map/reduce_scatter | solution.py:63
  136.7 0.8 copy-start.10
  136.7 11.2 %copy-start.2 = (s32[7168]{0:T(1024)S(1)}, s32[7168]{0:T(1024)}, u32[]{:S(2)}) copy-start(s32[7168]{0:T(1024)} %param.17) | copy-start | bytes 86020
  136.7 16.4 %copy-start.3 = (s32[7168]{0:T(1024)S(1)}, s32[7168]{0:T(1024)}, u32[]{:S(2)}) copy-start(s32[7168]{0:T(1024)} %param.16) | copy-start | bytes 86020
  136.7 117.2 %all-gather.5.cloned.1.call-start = ((), (), s32[]{:S(2)}) async-start(), calls=%async_computation.4 | async-start | bytes 4128768 | tf_op jit(solution)/shard_map/all_gather | solution.py:90
  203.9 1.6 copy-start.5
  204.0 1.6 copy-start.6
  205.5 5.4 %copy-start.7 = (pred[896,896]{0,1:T(8,128)(4,1)S(1)}, pred[896,896]{0,1:T(8,128)(4,1)}, u32[]{:S(2)}) copy-start(pred[896,896]{0,1:T(8,128)(4,1)} %compare_and_fusion) | copy-start | bytes 2408452
  218.8 35.1 %copy-start.9 = (s32[7168]{0:T(1024)S(1)}, s32[7168]{0:T(1024)}, u32[]{:S(2)}) copy-start(s32[7168]{0:T(1024)} %get-tuple-element.37) | copy-start | bytes 86020
  223.3 149.7 %reduce-scatter.5.cloned.1.call-start = ((), (), s32[]{:S(2)}) async-start(), calls=%async_computation.5 | async-start | bytes 7798784 | tf_op jit(solution)/shard_map/reduce_scatter | solution.py:91
  253.9 29.8 %copy-start.8 = (bf16[256,512]{1,0:T(8,128)(2,1)S(1)}, bf16[256,512]{1,0:T(8,128)(2,1)}, u32[]{:S(2)}) copy-start(bf16[256,512]{1,0:T(8,128)(2,1)} %param.14) | copy-start | bytes 786436
  283.7 91.3 %copy-start.1 = (bf16[512,768]{1,0:T(8,128)(2,1)S(1)}, bf16[512,768]{1,0:T(8,128)(2,1)}, u32[]{:S(2)}) copy-start(bf16[512,768]{1,0:T(8,128)(2,1)} %param.13) | copy-start | bytes 2359300
  290.8 82.2 %copy-start.4 = (bf16[448,512]{1,0:T(8,128)(2,1)S(1)}, bf16[448,512]{1,0:T(8,128)(2,1)}, u32[]{:S(2)}) copy-start(bf16[448,512]{1,0:T(8,128)(2,1)} %param.10) | copy-start | bytes 1376260
  290.8 82.2 %copy-start.11 = (f32[512]{0:T(512)S(1)}, f32[512]{0:T(512)}, u32[]{:S(2)}) copy-start(f32[512]{0:T(512)} %param.15) | copy-start | bytes 6148
Sparse Core Ops, SparseCore 0:
  23.3 68.2 all-gather.2
  136.8 64.0 reduce-scatter.2
  223.5 30.3 all-gather.4
  291.0 82.0 reduce-scatter.4
where the time goes:
time: 382 us; the launch traced here: 381 us
  waiting for transfers between devices  191 us (50%)
  local copies, waits for them, and re-layouts  121 us (32%)
  matrix products  29.9 us (8%)
  between operations  13.4 us (4%)
  blocking collectives  13.2 us (3%)
  other arithmetic  12.5 us (3%)
    reduce_scatter x1, waiting for transfers between devices, local(): lax.psum_scatter(jnp.dot(all_slots[owner_slot], w_out, preferred_element_...  82.2 us
    all_gather x1, waiting for transfers between devices, local(): gathered = lax.all_gather(normed, 'col', axis=0, tiled=True)  40.2 us
    reduce_scatter x1, waiting for transfers between devices, local(): lax.psum_scatter(jnp.dot(placed, w_qkv, preferred_element_type=jnp.float3...  38.2 us
    gather x1, local copies, waits for them, and re-layouts, local(): placed = gathered[at_slot]  33.8 us
    all_gather x1, waiting for transfers between devices, local(): all_slots = lax.all_gather(attended, 'row', axis=0, tiled=True)  30.3 us
    gather x1, local copies, waits for them, and re-layouts, local(): all_slots[owner_slot]  29.8 us
    scatter x1, local copies, waits for them, and re-layouts, local(): at_slot = jnp.zeros((slot_count,), jnp.int32).at[owner_slot].set(jnp.aran...  26.8 us
    psum x1, blocking collectives, local(): lax.psum((jnp.sum(own_rows, axis=1), jnp.sum(own_rows * own_rows, axis=1)...  13.2 us
  transfers between devices with their start and end apart: 4, of which 4 were waited for; matrix products, arithmetic and copies ran while one was open for 14% of the time, Pallas kernels for 0%

commit v1 on v0

--- a/solution.py
+++ b/solution.py
@@ -52,46 +52,54 @@
     )
     normed = normalize(own_rows, totals, squares, ln_gain, ln_shift)
     gathered = lax.all_gather(normed, "col", axis=0, tiled=True)
-    slot_count = owner_slot.shape[0]
-    at_slot = (
-        jnp.zeros((slot_count,), jnp.int32)
-        .at[owner_slot]
-        .set(jnp.arange(slot_count, dtype=jnp.int32))
-    )
-    placed = gathered[at_slot]
-    group_rows = slot_count // lax.axis_size("row")
+    count = gathered.shape[0]
+    n_row = lax.axis_size("row")
+    me = lax.axis_index("row")
+    group_rows = count // n_row
     mixed = lax.psum_scatter(
-        jnp.dot(placed, w_qkv, preferred_element_type=jnp.float32).astype(jnp.bfloat16),
+        jnp.dot(gathered, w_qkv, preferred_element_type=jnp.float32).astype(jnp.bfloat16),
         "row",
         scatter_dimension=0,
         tiled=True,
     ).astype(jnp.float32)
     heads_here = w_qkv.shape[1] // (3 * HD)
     mixed = mixed.reshape(group_rows, heads_here, 3, HD)
-    my_slots = lax.dynamic_slice_in_dim(at_slot, lax.axis_index("row") * group_rows, group_rows, 0)
-    row_pos = coords[0][my_slots].astype(jnp.float32)
-    col_pos = coords[1][my_slots].astype(jnp.float32)
-    seg_rows = segments[my_slots]
-    live_rows = present[my_slots]
+    halo = group_rows // 2
+
+    def own(values, before=0, after=0):
+        padded = jnp.pad(values, (halo, halo), constant_values=-1)
+        start = me * group_rows + halo - before
+        return lax.dynamic_slice_in_dim(padded, start, group_rows + before + after, 0)
+
+    row_pos = own(coords[0]).astype(jnp.float32)
+    col_pos = own(coords[1]).astype(jnp.float32)
+    seg_rows = own(segments)
+    live_rows = own(present)
+    seg_keys = own(segments, halo, halo)
+    live_keys = own(present, halo, halo)
     query_rows = rotate(mixed[:, :, 0], row_pos, col_pos).astype(jnp.bfloat16)
     key_rows = rotate(mixed[:, :, 1], row_pos, col_pos).astype(jnp.bfloat16)
     values = mixed[:, :, 2].astype(jnp.bfloat16)
+    both = jnp.stack([key_rows, values])
+    up = [(k, (k + 1) % n_row) for k in range(n_row)]
+    down = [((k + 1) % n_row, k) for k in range(n_row)]
+    before = lax.ppermute(both[:, group_rows - halo :], "row", up)
+    after = lax.ppermute(both[:, :halo], "row", down)
+    both = jnp.concatenate([before, both, after], axis=1)
     scores = jnp.einsum(
-        "qhe,khe->hqk", query_rows, key_rows, preferred_element_type=jnp.float32
+        "qhe,khe->hqk", query_rows, both[0], preferred_element_type=jnp.float32
     ) * HD ** (-0.5)
-    allowed = (seg_rows[:, None] == seg_rows[None, :]) & (live_rows[None, :] == 1)
+    allowed = (seg_rows[:, None] == seg_keys[None, :]) & (live_keys[None, :] == 1)
     scores = jnp.where(allowed[None], scores, -1e30)
     highest = jnp.max(scores, axis=-1, keepdims=True)
     weights = jnp.exp(scores - highest)
     probability = (weights / jnp.sum(weights, axis=-1, keepdims=True)).astype(jnp.bfloat16)
-    result = jnp.einsum("hqk,khe->qhe", probability, values, preferred_element_type=jnp.float32)
+    result = jnp.einsum("hqk,khe->qhe", probability, both[1], preferred_element_type=jnp.float32)
     attended = (result * live_rows[:, None, None].astype(jnp.float32)).astype(jnp.bfloat16)
     attended = attended.reshape(group_rows, heads_here * HD)
-    all_slots = lax.all_gather(attended, "row", axis=0, tiled=True)
+    all_tokens = lax.all_gather(attended, "row", axis=0, tiled=True)
     projected = lax.psum_scatter(
-        jnp.dot(all_slots[owner_slot], w_out, preferred_element_type=jnp.float32).astype(
-            jnp.bfloat16
-        ),
+        jnp.dot(all_tokens, w_out, preferred_element_type=jnp.float32).astype(jnp.bfloat16),
         "col",
         scatter_dimension=0,
         tiled=True,

time: 382 us -> 334 us (0.87)
  local copies, waits for them, and re-layouts: 121 us -> 6.86 us
  waiting for transfers between devices: 191 us -> 247 us
  matrix products: 29.9 us -> 37.7 us
    gather x6 -> x0, local copies, waits for them, and re-layouts: 84.2 us -> none  [the longest x1 33.8 us: local(): placed = gathered[at_slot]]
    all_gather x1, waiting for transfers between devices: 40.2 us -> 68.3 us  [local(): gathered = lax.all_gather(normed, 'col', axis=0, tiled=True)]
    scatter x1 -> x0, local copies, waits for them, and re-layouts: 26.8 us -> none  [local(): at_slot = jnp.zeros((slot_count,), jnp.int32).at[owner_slot].set(jnp.aran...]
    reduce_scatter x2, waiting for transfers between devices: 120 us -> 140 us  [the longest x1 82.4 us: local(): lax.psum_scatter(jnp.dot(all_tokens, w_out, preferred_element_type=jnp.fl...]
    ppermute x0 -> x2, waiting for transfers between devices: none -> 5.71 us  [the longest x1 2.92 us: local(): before = lax.ppermute(both[:, group_rows - halo:], 'row', up)]
    dot_general x3, matrix products: 22 us -> 26.3 us  [the longest x1 11.5 us: local(): jnp.dot(gathered, w_qkv, preferred_element_type=jnp.float32)]
  transfers between devices with their start and end apart: 4 -> 6, of which waited for: 4 -> 6; matrix products, arithmetic and copies ran while one was open for 14% -> 2% of each run, Pallas kernels for 0% -> 0%
where the time goes in v1:
time: 334 us; the launch traced here: 333 us
  waiting for transfers between devices  247 us (74%)
  matrix products  37.7 us (11%)
  other arithmetic  13.6 us (4%)
  between operations  13.3 us (4%)
  blocking collectives  13.2 us (4%)
  local copies, waits for them, and re-layouts  6.86 us (2%)
    reduce_scatter x1, waiting for transfers between devices, local(): lax.psum_scatter(jnp.dot(all_tokens, w_out, preferred_element_type=jnp.fl...  82.4 us
    all_gather x1, waiting for transfers between devices, local(): gathered = lax.all_gather(normed, 'col', axis=0, tiled=True)  68.3 us
    reduce_scatter x1, waiting for transfers between devices, local(): lax.psum_scatter(jnp.dot(gathered, w_qkv, preferred_element_type=jnp.floa...  58 us
    all_gather x1, waiting for transfers between devices, local(): all_tokens = lax.all_gather(attended, 'row', axis=0, tiled=True)  33 us
    psum x1, blocking collectives, local(): lax.psum((jnp.sum(own_rows, axis=1), jnp.sum(own_rows * own_rows, axis=1)...  13.2 us
    dot_general x1, matrix products, local(): jnp.dot(gathered, w_qkv, preferred_element_type=jnp.float32)  11.5 us
    sub x1, matrix products, local(): weights = jnp.exp(scores - highest)  11.4 us
    dot_general x1, matrix products, local(): jnp.einsum('hqk,khe->qhe', probability, both[1], preferred_element_type=j...  7.72 us
  transfers between devices with their start and end apart: 6, of which 6 were waited for; matrix products, arithmetic and copies ran while one was open for 2% of the time, Pallas kernels for 0%

profile of v1, /device:TPU:1, one launch (start us, length us, event | category | flops | bytes accessed | tf_op | source)
XLA Modules:
  0.0 333.4 jit_solution(2135108857201881790)
XLA Ops:
  6.5 0.0 copy-start
  6.5 0.0 all-gather.3.cloned.1.call-start
  6.5 1.3 convert_reduce_fusion
  7.9 13.2 %all-reduce.4 = (f32[448]{0:T(512)S(1)}, f32[448]{0:T(512)S(1)}) all-reduce(f32[448]{0:T(512)S(1)} %get-tuple-element.6, f32[448]{0:T(512)S(1)} %get-tuple-element.5), channel_id=1, replica_groups=mesh['row'=8,'col'=16] {'row'}, use_global_device_ids=true, to_apply=%region_3.0 | all-reduce | flops 896 | bytes 7168 | tf_op jit(solution)/shard_map/psum | solution.py:50
  21.1 2.0 fusion.13
  23.1 0.0 all-gather.3.cloned.1.call-update
  23.1 0.0 reduce-scatter.3.cloned.1.call-start
  23.2 68.3 %all-gather.3.cloned.1.call-done = bf16[7168,512]{1,0:T(8,128)(2,1)} async-done(((bf16[448,512]{1,0:T(8,128)(2,1)}), bf16[7168,512]{1,0:T(8,128)(2,1)}) %all-gather.3.cloned.1.call-update) | async-done | bytes 7340048 | tf_op jit(solution)/shard_map/all_gather | solution.py:54
  91.5 0.0 copy-done
  91.5 11.5 %convolution_convert_fusion = bf16[7168,768]{1,0:T(8,128)(2,1)} fusion(bf16[7168,512]{1,0:T(8,128)(2,1)} %all-gather.3.cloned.1.call-done, bf16[512,768]{1,0:T(8,128)(2,1)S(1)} %copy-done), kind=kOutput, calls=%fused_computation.4 | convolution fusion | flops 5642649600 | bytes 19136512 | tf_op jit(solution)/shard_map/dot_general | solution.py:60
  103.0 0.0 copy-start.7
  103.0 0.0 copy-start.6
  103.0 0.0 copy-start.8
  103.0 0.0 reduce-scatter.3.cloned.1.call-update
  103.0 0.0 all-gather.5.cloned.1.call-start
  103.1 0.6 copy-done.7
  103.7 0.1 fusion.19
  103.8 0.0 copy-done.6
  103.8 0.1 pad_dynamic-slice_fusion.2
  103.9 0.1 pad_dynamic-slice_fusion.3
  104.0 0.0 copy-done.8
  104.0 0.1 fusion.20
  104.1 0.3 broadcast_multiply_fusion.1
  104.4 2.6 fusion.18
  107.0 2.3 compare_and_fusion
  109.3 58.0 %reduce-scatter.3.cloned.1.call-done = bf16[896,768]{1,0:T(8,128)(2,1)} async-done(((bf16[7168,768]{1,0:T(8,128)(2,1)}), bf16[896,768]{1,0:T(8,128)(2,1)}) %reduce-scatter.3.cloned.1.call-update) | async-done | bytes 1376272 | tf_op jit(solution)/shard_map/reduce_scatter | solution.py:59
  167.3 1.8 copy.13
  169.1 0.8 copy.14
  169.9 0.2 reshape.195
  170.2 0.1 slice_bitcast_fusion.4
  170.3 0.0 copy-start.3
  170.3 0.0 copy-start.4
  170.3 1.5 fusion.26
  171.9 0.0 copy-done.3
  171.9 0.0 copy-done.4
  171.9 1.0 subtract_convert_fusion.1
  172.9 0.2 slice_bitcast_fusion.15
  173.1 0.2 slice_bitcast_fusion.14
  173.3 0.6 pad_maximum_fusion.3
  173.9 0.1 fusion.25
  174.0 0.0 collective-permute-start
  174.0 1.2 collective-permute-start.1
  175.2 0.2 fusion.28
  175.4 1.1 fusion.29
  176.5 2.9 collective-permute-done
  179.4 2.8 collective-permute-done.1
  182.2 1.0 pad_maximum_fusion
  183.2 11.4 %fusion.31 = (f32[2,896]{1,0:T(2,128)S(1)}, f32[2,896,1792]{2,1,0:T(8,128)}) fusion(pred[896,1792]{1,0:T(8,128)(4,1)} %compare_and_fusion, bf16[2,1792,2,128]{3,1,2,0:T(8,128)(2,1)S(1)} %pad_maximum_fusion, bf16[896,2,32]{2,0,1:T(8,128)(2,1)} %get-tuple-element.36, bf16[896,2,32]{2,0,1:T(8,128)(2,1)S(1)} %get-tuple-element.34, ...), kind=kOutput, calls=%fused_computation.72 | convolution fusion | flops 836765440 | bytes 16522240 | tf_op jit(solution)/shard_map/sub | solution.py:95
  194.6 0.0 copy-start.5
  194.6 7.7 %fusion.9 = bf16[2,128,896]{2,1,0:T(8,128)(2,1)} fusion(f32[2,896,1792]{2,1,0:T(8,128)} %get-tuple-element.44, f32[2,896]{1,0:T(2,128)S(1)} %get-tuple-element.43, bf16[2,1792,2,128]{3,1,2,0:T(8,128)(2,1)S(1)} %pad_maximum_fusion, f32[896]{0:T(1024)S(1)} %get-tuple-element.50), kind=kOutput, calls=%fused_computation.19 | convolution fusion | flops 828964864 | bytes 14232576 | tf_op jit(solution)/shard_map/hqk,khe->qhe/dot_general | solution.py:97
  202.4 0.0 all-gather.5.cloned.1.call-update
  202.4 0.0 reduce-scatter.5.cloned.1.call-start
  202.4 33.0 %all-gather.5.cloned.1.call-done = bf16[7168,256]{0,1:T(8,128)(2,1)} async-done(((bf16[896,256]{0,1:T(8,128)(2,1)}), bf16[7168,256]{0,1:T(8,128)(2,1)}) %all-gather.5.cloned.1.call-update) | async-done | bytes 3670032 | tf_op jit(solution)/shard_map/all_gather | solution.py:100
  235.4 0.0 copy-done.5
  235.4 7.1 %convolution_convert_fusion.1 = bf16[7168,512]{1,0:T(8,128)(2,1)} fusion(bf16[7168,256]{0,1:T(8,128)(2,1)} %all-gather.5.cloned.1.call-done, bf16[256,512]{1,0:T(8,128)(2,1)S(1)} %copy-done.5), kind=kOutput, calls=%fused_computation.5 | convolution fusion | flops 1882718208 | bytes 11272192 | tf_op jit(solution)/shard_map/dot_general | solution.py:102
  242.5 0.0 copy-start.1
  242.5 0.0 copy-start.2
  242.6 0.0 copy-start.9
  242.6 0.0 reduce-scatter.5.cloned.1.call-update
  242.6 82.4 %reduce-scatter.5.cloned.1.call-done = bf16[448,512]{1,0:T(8,128)(2,1)} async-done(((bf16[7168,512]{1,0:T(8,128)(2,1)}), bf16[448,512]{1,0:T(8,128)(2,1)}) %reduce-scatter.5.cloned.1.call-update) | async-done | bytes 458768 | tf_op jit(solution)/shard_map/reduce_scatter | solution.py:101
  324.9 0.0 copy-done.2
  324.9 0.0 copy-done.9
  325.0 1.9 fusion.15
  326.9 0.0 copy-done.1
  (4 shorter events, 0.1 us)
Async XLA Ops:
  6.5 85.0 %copy-start = (bf16[512,768]{1,0:T(8,128)(2,1)S(1)}, bf16[512,768]{1,0:T(8,128)(2,1)}, u32[]{:S(2)}) copy-start(bf16[512,768]{1,0:T(8,128)(2,1)} %param.13) | copy-start | bytes 2359300
  6.5 85.0 %all-gather.3.cloned.1.call-start = ((), (), s32[]{:S(2)}) async-start(), calls=%async_computation.2 | async-start | bytes 7798784 | tf_op jit(solution)/shard_map/all_gather | solution.py:54
  23.1 144.1 %reduce-scatter.3.cloned.1.call-start = ((), (), s32[]{:S(2)}) async-start(), calls=%async_computation.3 | async-start | bytes 12386304 | tf_op jit(solution)/shard_map/reduce_scatter | solution.py:59
  103.0 0.7 copy-start.7
  103.0 0.8 copy-start.6
  103.0 1.0 copy-start.8
  103.0 132.4 %all-gather.5.cloned.1.call-start = ((), (), s32[]{:S(2)}) async-start(), calls=%async_computation.4 | async-start | bytes 4128768 | tf_op jit(solution)/shard_map/all_gather | solution.py:100
  170.3 1.6 copy-start.3
  170.3 1.6 copy-start.4
  174.0 5.4 %collective-permute-start = (bf16[2,448,2,128]{3,1,2,0:T(8,128)(2,1)S(1)}, bf16[2,448,2,128]{3,1,2,0:T(8,128)(2,1)S(1)}, u32[]{:S(2)}, u32[]{:S(2)}) collective-permute-start(bf16[2,448,2,128]{3,1,2,0:T(8,128)(2,1)S(1)} %get-tuple-element.15), channel_id=1, source_target_pairs={{0,16},{16,32},{32,48},{48,64},{64,80},{80,96},{96,112},{112,0},{1... | collective-permute-start | bytes 1376264 | tf_op jit(solution)/shard_map/ppermute | solution.py:86
  174.0 8.2 %collective-permute-start.1 = (bf16[2,448,2,128]{3,1,2,0:T(8,128)(2,1)S(1)}, bf16[2,448,2,128]{3,1,2,0:T(8,128)(2,1)S(1)}, u32[]{:S(2)}, u32[]{:S(2)}) collective-permute-start(bf16[2,448,2,128]{3,1,2,0:T(8,128)(2,1)S(1)} %get-tuple-element.16), channel_id=1, source_target_pairs={{16,0},{32,16},{48,32},{64,48},{80,64},{96,80},{112,96},{0,112},{1... | collective-permute-start | bytes 1376264 | tf_op jit(solution)/shard_map/ppermute | solution.py:87
  194.6 40.8 %copy-start.5 = (bf16[256,512]{1,0:T(8,128)(2,1)S(1)}, bf16[256,512]{1,0:T(8,128)(2,1)}, u32[]{:S(2)}) copy-start(bf16[256,512]{1,0:T(8,128)(2,1)} %param.14) | copy-start | bytes 786436
  202.4 122.6 %reduce-scatter.5.cloned.1.call-start = ((), (), s32[]{:S(2)}) async-start(), calls=%async_computation.5 | async-start | bytes 7798784 | tf_op jit(solution)/shard_map/reduce_scatter | solution.py:101
  242.5 84.3 %copy-start.1 = (bf16[512,768]{1,0:T(8,128)(2,1)S(1)}, bf16[512,768]{1,0:T(8,128)(2,1)}, u32[]{:S(2)}) copy-start(bf16[512,768]{1,0:T(8,128)(2,1)} %param.13) | copy-start | bytes 2359300
  242.5 82.4 %copy-start.2 = (bf16[448,512]{1,0:T(8,128)(2,1)S(1)}, bf16[448,512]{1,0:T(8,128)(2,1)}, u32[]{:S(2)}) copy-start(bf16[448,512]{1,0:T(8,128)(2,1)} %param.10) | copy-start | bytes 1376260
  242.6 82.4 %copy-start.9 = (f32[512]{0:T(512)S(1)}, f32[512]{0:T(512)}, u32[]{:S(2)}) copy-start(f32[512]{0:T(512)} %param.15) | copy-start | bytes 6148
Sparse Core Ops, SparseCore 0:
  23.3 68.2 all-gather.2
  103.1 64.1 reduce-scatter.2
  202.5 32.8 all-gather.4
  242.7 82.2 reduce-scatter.4
